TPU v7x, 256 devices: a whole 4x4x8 slice. The times are simulated.
256 devices in a mesh: subj: 4 (over y_hi, core), slab: 64 (over x, z, y_lo).
Axes of the slice: x: 4, y: 4 (y_hi: 2, y_lo: 2; y = y_hi * 2 + y_lo), z: 8, core: 2. Of those that a mesh axis runs over, the one named last changes fastest.
Arguments:
- momentum: bfloat16 [4, 3, 128, 256, 256], P('subj', None, 'slab'), may hold values from -6 to 6
- adjoint: bfloat16 [4, 128, 256, 256], P('subj', 'slab'), may hold values from -6 to 6
- code: int32 [4, 128, 256, 256], P('subj', 'slab'), may hold values from 0 to 4095
- template_grad: bfloat16 [3, 128, 256, 256], P(None, 'slab'), may hold values from -6 to 6
Outputs:
- alignment: bfloat16 [4, 128, 256, 256], P('subj', 'slab')
- template_update: float32 [128, 256, 256], P('slab', 'subj')
Inputs may be any that keep to these rules, and one draw needn't show every extreme that they name: code // 256, (code // 16) % 16 and code % 16 are each 8 plus a displacement along z, y and x in quarter voxels.
All inputs are finite; a program needn't handle non-finite values.
Results may differ from a plain program's by a relative error of at most 0.012.
Values may be sent and summed in bfloat16 or wider, within the bound.
A program may use at most 128 MiB of HBM per device.

v0:
```python
import jax
import jax.numpy as jnp
from jax import lax
from jax.sharding import PartitionSpec as P

rim = 2
bias = 8
decay = 8.0


def padded(cells, sides, width):
    for axis, dim in sides:
        count = lax.axis_size(axis)
        ends = count - 1
        head = lax.slice_in_dim(cells, 0, width, axis=dim)
        tail = lax.slice_in_dim(cells, cells.shape[dim] - width, cells.shape[dim], axis=dim)
        cells = jnp.concatenate(
            [
                lax.ppermute(tail, axis, [(i, (i + 1) % count) for i in range(ends)]),
                cells,
                lax.ppermute(head, axis, [((i + 1) % count, i) for i in range(ends)]),
            ],
            axis=dim,
        )
    return cells


def from_behind(value, axis, steps):
    count = lax.axis_size(axis)
    first, last = (max(0, -steps), min(count, count - steps))
    return lax.ppermute(value, axis, [(source, source + steps) for source in range(first, last)])


def taps_matrix(rows, cols, offset):
    lags = jnp.arange(-15, 16, dtype=jnp.int32).astype(jnp.float32)
    scale = jnp.sqrt(jnp.sum(jnp.exp(-2.0 * jnp.abs(lags) / decay)))
    lag = (
        jnp.arange(rows, dtype=jnp.int32)[:, None]
        - offset
        - jnp.arange(cols, dtype=jnp.int32)[None, :]
    )
    dist = jnp.abs(lag).astype(jnp.float32)
    return jnp.where(jnp.abs(lag) <= 15, jnp.exp(-dist / decay) / scale, 0.0).astype(jnp.bfloat16)


def axis_weights(shift):
    whole = shift // 4
    frac = (shift - 4 * whole).astype(jnp.float32) * 0.25
    weights = []
    for offset in range(-rim, rim + 1):
        lower = jnp.where(whole == offset, 1.0 - frac, 0.0)
        upper = jnp.where(whole + 1 == offset, frac, 0.0)
        weights.append(lower + upper)
    return weights


def transport(framed, encoded):
    depth, height, breadth = encoded.shape
    weights_z = axis_weights(encoded // 256 - bias)
    weights_y = axis_weights(encoded // 16 % 16 - bias)
    weights_x = axis_weights(encoded % 16 - bias)
    pulled = jnp.zeros(encoded.shape, jnp.float32)
    for index_z in range(2 * rim + 1):
        plane_sum = jnp.zeros(encoded.shape, jnp.float32)
        for index_y in range(2 * rim + 1):
            row_sum = jnp.zeros(encoded.shape, jnp.float32)
            for index_x in range(2 * rim + 1):
                window = lax.slice(
                    framed,
                    (index_z, index_y, index_x),
                    (index_z + depth, index_y + height, index_x + breadth),
                )
                row_sum = row_sum + weights_x[index_x] * window.astype(jnp.float32)
            plane_sum = plane_sum + weights_y[index_y] * row_sum
        pulled = pulled + weights_z[index_z] * plane_sum
    return pulled


def per_device(momentum, adjoint, code, template_grad):
    subjects, _, depth, height, breadth = momentum.shape
    framed = padded(adjoint, (("slab", 1),), 2)
    framed = jnp.pad(framed, ((0, 0), (0, 0), (rim, rim), (rim, rim)))
    pulled = jax.vmap(transport)(framed, code)
    gradient = template_grad.astype(jnp.float32)
    mixed = (momentum.astype(jnp.float32) + pulled[:, None] * gradient[None]).astype(jnp.bfloat16)
    kernel_x = taps_matrix(breadth, breadth, 0)
    kernel_y = taps_matrix(height, height, 0)
    along_x = jnp.dot(mixed.reshape(-1, breadth), kernel_x, preferred_element_type=jnp.float32)
    along_x = along_x.astype(jnp.bfloat16).reshape(subjects * 3, depth, height, breadth)
    along_y = jnp.einsum("mznx,ny->mzyx", along_x, kernel_y, preferred_element_type=jnp.float32)
    along_y = along_y.astype(jnp.bfloat16).reshape(subjects * 3, depth, height * breadth)
    reach = (14 + depth) // depth
    below = []
    for distance in range(reach, 0, -1):
        start = max(0, distance * depth - 15)
        below.append(from_behind(along_y[:, start:], "slab", distance))
    above = []
    for distance in range(1, reach + 1):
        count = min(depth, 15 - (distance - 1) * depth)
        above.append(from_behind(along_y[:, :count], "slab", -distance))
    stacked = jnp.concatenate(below + [along_y] + above, axis=1)
    kernel_z = taps_matrix(depth + 30, depth, 15)
    velocity = jnp.einsum(
        "mlq,lz->mzq", stacked, kernel_z, preferred_element_type=jnp.float32
    ).astype(jnp.bfloat16)
    velocity = velocity.reshape(subjects, 3, depth, height, breadth)
    product = jnp.sum(gradient[None] * velocity.astype(jnp.float32), axis=1)
    alignment = product.astype(jnp.bfloat16)
    partial_sum = jnp.sum(pulled * (1.0 + product), axis=0)
    template_update = lax.psum_scatter(partial_sum, "subj", scatter_dimension=1, tiled=True)
    return (alignment, template_update)


def solution(mesh):
    return jax.shard_map(
        per_device,
        mesh=mesh,
        in_specs=(
            P("subj", None, "slab", None, None),
            P("subj", "slab", None, None),
            P("subj", "slab", None, None),
            P(None, "slab", None, None),
        ),
        out_specs=(P("subj", "slab", None, None), P("slab", "subj", None)),
        check_vma=False,
    )
```

profile of v0, /device:TPU:1, one launch (start us, length us, event | category | flops | bytes accessed | tf_op | source)
XLA Modules:
  0.0 778.8 jit_solution(2909148212200459193)
XLA Ops:
  7.2 4.2 collective-permute-start
  11.4 1.3 collective-permute-start.1
  12.7 0.6 exponential_reduce_fusion
  14.0 2.7 collective-permute-done
  16.8 3.8 collective-permute-done.1
  20.5 1.8 select_maximum_fusion
  22.4 16.3 %multiply_add_fusion = f32[1,2,256,256]{3,2,1,0:T(8,128)S(1)} fusion(bf16[1,2,256,256]{3,2,1,0:T(8,128)(2,1)S(1)} %collective-permute-done.1, bf16[1,2,256,256]{3,2,1,0:T(8,128)(2,1)S(1)} %copy-done.3, bf16[1,2,256,256]{3,2,1,0:T(8,128)(2,1)S(1)} %collective-permute-done, s32[1,2,256,256]{3,2,1,0:T(8,128)S(1)} %copy-done.15, ...), kind=kLoop, calls=%fused_computation.57 | loop fusion | flops 77463552 | bytes 33292288 | tf_op jit(solution)/shard_map/vmap()/add | solution.py:75
  38.7 0.3 fusion.7
  39.0 0.4 convolution_convert_fusion.1
  39.4 0.1 copy-done
  39.4 0.4 fusion.9
  39.8 0.3 reshape.51
  40.1 1.1 fusion.59
  41.2 0.5 copy.6
  41.7 14.6 %collective-permute-start.2 = (bf16[3,1,65536]{2,0,1:T(4,128)(2,1)S(1)}, bf16[3,1,65536]{2,0,1:T(4,128)(2,1)S(1)}, u32[]{:S(2)}, u32[]{:S(2)}) collective-permute-start(bf16[3,1,65536]{2,0,1:T(4,128)(2,1)S(1)} %copy.6), channel_id=1, source_target_pairs={{0,8},{1,9},{2,10},{3,11},{4,12},{5,13},{6,14},{7,15},{8,16},{9,17... | collective-permute-start | bytes 1179656 | tf_op jit(solution)/shard_map/ppermute | solution.py:31
  56.3 1.3 collective-permute-start.10
  57.6 1.3 collective-permute-start.11
  58.9 1.3 collective-permute-start.12
  60.2 1.3 collective-permute-start.13
  61.5 0.5 copy.7
  62.0 12.1 %collective-permute-done.2 = bf16[3,1,65536]{2,0,1:T(4,128)(2,1)S(1)} collective-permute-done((bf16[3,1,65536]{2,0,1:T(4,128)(2,1)S(1)}, bf16[3,1,65536]{2,0,1:T(4,128)(2,1)S(1)}, u32[]{:S(2)}, u32[]{:S(2)}) %collective-permute-start.2) | collective-permute-done | bytes 393248 | tf_op jit(solution)/shard_map/ppermute | solution.py:31
  74.2 1.3 collective-permute-start.17
  75.5 14.3 %collective-permute-done.17 = bf16[3,1,65536]{2,0,1:T(4,128)(2,1)S(1)} collective-permute-done((bf16[3,1,65536]{2,0,1:T(4,128)(2,1)S(1)}, bf16[3,1,65536]{2,0,1:T(4,128)(2,1)S(1)}, u32[]{:S(2)}, u32[]{:S(2)}) %collective-permute-start.17) | collective-permute-done | bytes 393248 | tf_op jit(solution)/shard_map/ppermute | solution.py:31
  89.8 1.3 collective-permute-start.14
  91.1 1.3 collective-permute-start.15
  92.4 20.0 %collective-permute-done.11 = bf16[3,2,65536]{2,1,0:T(2,128)(2,1)} collective-permute-done((bf16[3,2,65536]{2,1,0:T(2,128)(2,1)S(1)}, bf16[3,2,65536]{2,1,0:T(2,128)(2,1)}, u32[]{:S(2)}, u32[]{:S(2)}) %collective-permute-start.11) | collective-permute-done | bytes 786464 | tf_op jit(solution)/shard_map/ppermute | solution.py:31
  112.4 1.3 collective-permute-start.16
  113.7 167.0 %collective-permute-start.3 = (bf16[3,2,65536]{2,1,0:T(2,128)(2,1)S(1)}, bf16[3,2,65536]{2,1,0:T(2,128)(2,1)S(1)}, u32[]{:S(2)}, u32[]{:S(2)}) collective-permute-start(bf16[3,2,65536]{2,1,0:T(2,128)(2,1)S(1)} %reshape.51), channel_id=1, source_target_pairs={{0,7},{1,8},{2,9},{3,10},{4,11},{5,12},{6,13},{7,14},{8,15},{9,16}... | collective-permute-start | bytes 2359304 | tf_op jit(solution)/shard_map/ppermute | solution.py:31
  280.7 6.4 collective-permute-start.4
  287.2 9.5 %collective-permute-start.5 = (bf16[3,2,65536]{2,1,0:T(2,128)(2,1)S(1)}, bf16[3,2,65536]{2,1,0:T(2,128)(2,1)S(1)}, u32[]{:S(2)}, u32[]{:S(2)}) collective-permute-start(bf16[3,2,65536]{2,1,0:T(2,128)(2,1)S(1)} %reshape.51), channel_id=1, source_target_pairs={{0,5},{1,6},{2,7},{3,8},{4,9},{5,10},{6,11},{7,12},{8,13},{9,14},{... | collective-permute-start | bytes 2359304 | tf_op jit(solution)/shard_map/ppermute | solution.py:31
  296.7 27.2 %collective-permute-start.6 = (bf16[3,2,65536]{2,1,0:T(2,128)(2,1)S(1)}, bf16[3,2,65536]{2,1,0:T(2,128)(2,1)S(1)}, u32[]{:S(2)}, u32[]{:S(2)}) collective-permute-start(bf16[3,2,65536]{2,1,0:T(2,128)(2,1)S(1)} %reshape.51), channel_id=1, source_target_pairs={{0,4},{1,5},{2,6},{3,7},{4,8},{5,9},{6,10},{7,11},{8,12},{9,13},{1... | collective-permute-start | bytes 2359304 | tf_op jit(solution)/shard_map/ppermute | solution.py:31
  323.9 17.8 %collective-permute-done.16 = bf16[3,2,65536]{2,1,0:T(2,128)(2,1)S(1)} collective-permute-done((bf16[3,2,65536]{2,1,0:T(2,128)(2,1)S(1)}, bf16[3,2,65536]{2,1,0:T(2,128)(2,1)S(1)}, u32[]{:S(2)}, u32[]{:S(2)}) %collective-permute-start.16) | collective-permute-done | bytes 786464 | tf_op jit(solution)/shard_map/ppermute | solution.py:31
  341.7 38.9 %collective-permute-start.7 = (bf16[3,2,65536]{2,1,0:T(2,128)(2,1)S(1)}, bf16[3,2,65536]{2,1,0:T(2,128)(2,1)S(1)}, u32[]{:S(2)}, u32[]{:S(2)}) collective-permute-start(bf16[3,2,65536]{2,1,0:T(2,128)(2,1)S(1)} %reshape.51), channel_id=1, source_target_pairs={{0,3},{1,4},{2,5},{3,6},{4,7},{5,8},{6,9},{7,10},{8,11},{9,12},{10... | collective-permute-start | bytes 2359304 | tf_op jit(solution)/shard_map/ppermute | solution.py:31
  380.6 36.0 %collective-permute-start.8 = (bf16[3,2,65536]{2,1,0:T(2,128)(2,1)S(1)}, bf16[3,2,65536]{2,1,0:T(2,128)(2,1)S(1)}, u32[]{:S(2)}, u32[]{:S(2)}) collective-permute-start(bf16[3,2,65536]{2,1,0:T(2,128)(2,1)S(1)} %reshape.51), channel_id=1, source_target_pairs={{0,2},{1,3},{2,4},{3,5},{4,6},{5,7},{6,8},{7,9},{8,10},{9,11},{10,... | collective-permute-start | bytes 2359304 | tf_op jit(solution)/shard_map/ppermute | solution.py:31
  416.7 0.9 copy-done.9
  417.6 2.2 collective-permute-start.9
  419.8 0.7 copy.8
  420.5 0.7 copy.9
  421.2 25.5 %collective-permute-done.7 = bf16[3,2,65536]{2,1,0:T(2,128)(2,1)S(1)} collective-permute-done((bf16[3,2,65536]{2,1,0:T(2,128)(2,1)S(1)}, bf16[3,2,65536]{2,1,0:T(2,128)(2,1)S(1)}, u32[]{:S(2)}, u32[]{:S(2)}) %collective-permute-start.7) | collective-permute-done | bytes 786464 | tf_op jit(solution)/shard_map/ppermute | solution.py:31
  446.7 16.9 %collective-permute-done.8 = bf16[3,2,65536]{2,1,0:T(2,128)(2,1)S(1)} collective-permute-done((bf16[3,2,65536]{2,1,0:T(2,128)(2,1)S(1)}, bf16[3,2,65536]{2,1,0:T(2,128)(2,1)S(1)}, u32[]{:S(2)}, u32[]{:S(2)}) %collective-permute-start.8) | collective-permute-done | bytes 786464 | tf_op jit(solution)/shard_map/ppermute | solution.py:31
  463.6 0.9 copy-done.13
  464.5 210.5 %concatenate.15 = bf16[3,32,65536]{2,1,0:T(8,128)(2,1)} concatenate(bf16[3,1,65536]{2,1,0:T(2,128)(2,1)S(1)} %copy.8, bf16[3,2,65536]{2,1,0:T(2,128)(2,1)} %copy-done.8, bf16[3,2,65536]{2,1,0:T(2,128)(2,1)} %copy-done.9, bf16[3,2,65536]{2,1,0:T(2,128)(2,1)} %copy-done.10, bf16[3,2,65536]{2,1,0:T(2,128)(2,1)} %copy-done.11, bf16[3,2,65536]{2,1,0:T(2,128)(2,1)} %copy-done.12, ...), dimensions={1} | concatenate | bytes 25165824 | tf_op jit(solution)/shard_map/concatenate | solution.py:101
  675.0 6.3 fusion.1
  681.3 1.4 reshape.52
  682.8 1.4 fusion.8
  684.2 0.9 fusion.21
  685.1 0.7 convert_bitcast_fusion
  685.8 86.1 %reduce-scatter.2.cloned.1.call-done = f32[2,64,256]{2,1,0:T(8,128)} async-done(((f32[2,256,256]{2,1,0:T(8,128)}), f32[2,64,256]{2,1,0:T(8,128)}) %reduce-scatter.2.cloned.1.call-update) | async-done | bytes 131088 | tf_op jit(solution)/shard_map/reduce_scatter | solution.py:110
  (42 shorter events, 0.1 us)
Async XLA Ops:
  7.2 15.2 %copy-start.3 = (bf16[1,2,256,256]{3,2,1,0:T(8,128)(2,1)S(1)}, bf16[1,2,256,256]{3,2,1,0:T(8,128)(2,1)}, u32[]{:S(2)}) copy-start(bf16[1,2,256,256]{3,2,1,0:T(8,128)(2,1)} %param.5) | copy-start | bytes 786436
  7.2 15.2 %copy-start.15 = (s32[1,2,256,256]{3,2,1,0:T(8,128)S(1)}, s32[1,2,256,256]{3,2,1,0:T(8,128)}, u32[]{:S(2)}) copy-start(s32[1,2,256,256]{3,2,1,0:T(8,128)} %param.6) | copy-start | bytes 1572868
  7.2 764.8 %reduce-scatter.2.cloned.1.call-start = ((), (), s32[]{:S(2)}) async-start(), calls=%async_computation.1 | async-start | bytes 655360 | tf_op jit(solution)/shard_map/reduce_scatter | solution.py:110
  7.2 9.5 %collective-permute-start = (bf16[1,2,256,256]{3,2,1,0:T(8,128)(2,1)}, bf16[1,2,256,256]{3,2,1,0:T(8,128)(2,1)S(1)}, u32[]{:S(2)}, u32[]{:S(2)}) collective-permute-start(bf16[1,2,256,256]{3,2,1,0:T(8,128)(2,1)} %param.5), channel_id=1, source_target_pairs={{0,1},{1,2},{2,3},{3,4},{4,5},{5,6},{6,7},{7,8},{8,9},{9,10},{10,1... | collective-permute-start | bytes 786440 | tf_op jit(solution)/shard_map/ppermute | solution.py:19
  11.4 9.1 %collective-permute-start.1 = (bf16[1,2,256,256]{3,2,1,0:T(8,128)(2,1)}, bf16[1,2,256,256]{3,2,1,0:T(8,128)(2,1)S(1)}, u32[]{:S(2)}, u32[]{:S(2)}) collective-permute-start(bf16[1,2,256,256]{3,2,1,0:T(8,128)(2,1)} %param.5), channel_id=1, source_target_pairs={{1,0},{2,1},{3,2},{4,3},{5,4},{6,5},{7,6},{8,7},{9,8},{10,9},{11,1... | collective-permute-start | bytes 786440 | tf_op jit(solution)/shard_map/ppermute | solution.py:21
  22.4 16.3 %copy-start.2 = (bf16[3,2,256,256]{3,2,1,0:T(8,128)(2,1)S(1)}, bf16[3,2,256,256]{3,2,1,0:T(8,128)(2,1)}, u32[]{:S(2)}) copy-start(bf16[3,2,256,256]{3,2,1,0:T(8,128)(2,1)} %param.7) | copy-start | bytes 2359300
  22.4 16.3 %copy-start.14 = (bf16[1,3,2,256,256]{4,3,2,1,0:T(8,128)(2,1)S(1)}, bf16[1,3,2,256,256]{4,3,2,1,0:T(8,128)(2,1)}, u32[]{:S(2)}) copy-start(bf16[1,3,2,256,256]{4,3,2,1,0:T(8,128)(2,1)} %param.4) | copy-start | bytes 2359300
  38.7 0.8 copy-start
  41.7 32.4 %collective-permute-start.2 = (bf16[3,1,65536]{2,0,1:T(4,128)(2,1)S(1)}, bf16[3,1,65536]{2,0,1:T(4,128)(2,1)S(1)}, u32[]{:S(2)}, u32[]{:S(2)}) collective-permute-start(bf16[3,1,65536]{2,0,1:T(4,128)(2,1)S(1)} %copy.6), channel_id=1, source_target_pairs={{0,8},{1,9},{2,10},{3,11},{4,12},{5,13},{6,14},{7,15},{8,16},{9,17... | collective-permute-start | bytes 1179656 | tf_op jit(solution)/shard_map/ppermute | solution.py:31
  56.3 34.8 %collective-permute-start.10 = (bf16[3,2,65536]{2,1,0:T(2,128)(2,1)S(1)}, bf16[3,2,65536]{2,1,0:T(2,128)(2,1)S(1)}, u32[]{:S(2)}, u32[]{:S(2)}) collective-permute-start(bf16[3,2,65536]{2,1,0:T(2,128)(2,1)S(1)} %reshape.51), channel_id=1, source_target_pairs={{1,0},{2,1},{3,2},{4,3},{5,4},{6,5},{7,6},{8,7},{9,8},{10,9},{11,1... | collective-permute-start | bytes 2359304 | tf_op jit(solution)/shard_map/ppermute | solution.py:31
  57.6 54.8 %collective-permute-start.11 = (bf16[3,2,65536]{2,1,0:T(2,128)(2,1)S(1)}, bf16[3,2,65536]{2,1,0:T(2,128)(2,1)}, u32[]{:S(2)}, u32[]{:S(2)}) collective-permute-start(bf16[3,2,65536]{2,1,0:T(2,128)(2,1)S(1)} %reshape.51), channel_id=1, source_target_pairs={{2,0},{3,1},{4,2},{5,3},{6,4},{7,5},{8,6},{9,7},{10,8},{11,9},{12,... | collective-permute-start | bytes 2359304 | tf_op jit(solution)/shard_map/ppermute | solution.py:31
  58.9 54.8 %collective-permute-start.12 = (bf16[3,2,65536]{2,1,0:T(2,128)(2,1)S(1)}, bf16[3,2,65536]{2,1,0:T(2,128)(2,1)}, u32[]{:S(2)}, u32[]{:S(2)}) collective-permute-start(bf16[3,2,65536]{2,1,0:T(2,128)(2,1)S(1)} %reshape.51), channel_id=1, source_target_pairs={{3,0},{4,1},{5,2},{6,3},{7,4},{8,5},{9,6},{10,7},{11,8},{12,9},{13... | collective-permute-start | bytes 2359304 | tf_op jit(solution)/shard_map/ppermute | solution.py:31
  60.2 220.5 %collective-permute-start.13 = (bf16[3,2,65536]{2,1,0:T(2,128)(2,1)S(1)}, bf16[3,2,65536]{2,1,0:T(2,128)(2,1)S(1)}, u32[]{:S(2)}, u32[]{:S(2)}) collective-permute-start(bf16[3,2,65536]{2,1,0:T(2,128)(2,1)S(1)} %reshape.51), channel_id=1, source_target_pairs={{4,0},{5,1},{6,2},{7,3},{8,4},{9,5},{10,6},{11,7},{12,8},{13,9},{1... | collective-permute-start | bytes 2359304 | tf_op jit(solution)/shard_map/ppermute | solution.py:31
  74.2 15.6 %collective-permute-start.17 = (bf16[3,1,65536]{2,0,1:T(4,128)(2,1)S(1)}, bf16[3,1,65536]{2,0,1:T(4,128)(2,1)S(1)}, u32[]{:S(2)}, u32[]{:S(2)}) collective-permute-start(bf16[3,1,65536]{2,0,1:T(4,128)(2,1)S(1)} %copy.7), channel_id=1, source_target_pairs={{8,0},{9,1},{10,2},{11,3},{12,4},{13,5},{14,6},{15,7},{16,8},{17,9... | collective-permute-start | bytes 1179656 | tf_op jit(solution)/shard_map/ppermute | solution.py:31
  89.8 197.4 %collective-permute-start.14 = (bf16[3,2,65536]{2,1,0:T(2,128)(2,1)S(1)}, bf16[3,2,65536]{2,1,0:T(2,128)(2,1)S(1)}, u32[]{:S(2)}, u32[]{:S(2)}) collective-permute-start(bf16[3,2,65536]{2,1,0:T(2,128)(2,1)S(1)} %reshape.51), channel_id=1, source_target_pairs={{5,0},{6,1},{7,2},{8,3},{9,4},{10,5},{11,6},{12,7},{13,8},{14,9},{... | collective-permute-start | bytes 2359304 | tf_op jit(solution)/shard_map/ppermute | solution.py:31
  91.1 205.5 %collective-permute-start.15 = (bf16[3,2,65536]{2,1,0:T(2,128)(2,1)S(1)}, bf16[3,2,65536]{2,1,0:T(2,128)(2,1)S(1)}, u32[]{:S(2)}, u32[]{:S(2)}) collective-permute-start(bf16[3,2,65536]{2,1,0:T(2,128)(2,1)S(1)} %reshape.51), channel_id=1, source_target_pairs={{6,0},{7,1},{8,2},{9,3},{10,4},{11,5},{12,6},{13,7},{14,8},{15,9},... | collective-permute-start | bytes 2359304 | tf_op jit(solution)/shard_map/ppermute | solution.py:31
  112.4 229.3 %collective-permute-start.16 = (bf16[3,2,65536]{2,1,0:T(2,128)(2,1)S(1)}, bf16[3,2,65536]{2,1,0:T(2,128)(2,1)S(1)}, u32[]{:S(2)}, u32[]{:S(2)}) collective-permute-start(bf16[3,2,65536]{2,1,0:T(2,128)(2,1)S(1)} %reshape.51), channel_id=1, source_target_pairs={{7,0},{8,1},{9,2},{10,3},{11,4},{12,5},{13,6},{14,7},{15,8},{16,9}... | collective-permute-start | bytes 2359304 | tf_op jit(solution)/shard_map/ppermute | solution.py:31
  113.7 266.9 %collective-permute-start.3 = (bf16[3,2,65536]{2,1,0:T(2,128)(2,1)S(1)}, bf16[3,2,65536]{2,1,0:T(2,128)(2,1)S(1)}, u32[]{:S(2)}, u32[]{:S(2)}) collective-permute-start(bf16[3,2,65536]{2,1,0:T(2,128)(2,1)S(1)} %reshape.51), channel_id=1, source_target_pairs={{0,7},{1,8},{2,9},{3,10},{4,11},{5,12},{6,13},{7,14},{8,15},{9,16}... | collective-permute-start | bytes 2359304 | tf_op jit(solution)/shard_map/ppermute | solution.py:31
  280.7 139.1 %copy-start.4 = (bf16[3,2,65536]{2,1,0:T(2,128)(2,1)}, bf16[3,2,65536]{2,1,0:T(2,128)(2,1)S(1)}, u32[]{:S(2)}) copy-start(bf16[3,2,65536]{2,1,0:T(2,128)(2,1)S(1)} %collective-permute-done.13) | copy-start | bytes 2359300
  280.7 135.9 %collective-permute-start.4 = (bf16[3,2,65536]{2,1,0:T(2,128)(2,1)S(1)}, bf16[3,2,65536]{2,1,0:T(2,128)(2,1)S(1)}, u32[]{:S(2)}, u32[]{:S(2)}) collective-permute-start(bf16[3,2,65536]{2,1,0:T(2,128)(2,1)S(1)} %reshape.51), channel_id=1, source_target_pairs={{0,6},{1,7},{2,8},{3,9},{4,10},{5,11},{6,12},{7,13},{8,14},{9,15},... | collective-permute-start | bytes 2359304 | tf_op jit(solution)/shard_map/ppermute | solution.py:31
  287.2 132.6 %copy-start.5 = (bf16[3,2,65536]{2,1,0:T(2,128)(2,1)}, bf16[3,2,65536]{2,1,0:T(2,128)(2,1)S(1)}, u32[]{:S(2)}) copy-start(bf16[3,2,65536]{2,1,0:T(2,128)(2,1)S(1)} %collective-permute-done.14) | copy-start | bytes 2359300
  287.2 134.0 %collective-permute-start.5 = (bf16[3,2,65536]{2,1,0:T(2,128)(2,1)S(1)}, bf16[3,2,65536]{2,1,0:T(2,128)(2,1)S(1)}, u32[]{:S(2)}, u32[]{:S(2)}) collective-permute-start(bf16[3,2,65536]{2,1,0:T(2,128)(2,1)S(1)} %reshape.51), channel_id=1, source_target_pairs={{0,5},{1,6},{2,7},{3,8},{4,9},{5,10},{6,11},{7,12},{8,13},{9,14},{... | collective-permute-start | bytes 2359304 | tf_op jit(solution)/shard_map/ppermute | solution.py:31
  296.7 120.0 %copy-start.6 = (bf16[3,2,65536]{2,1,0:T(2,128)(2,1)}, bf16[3,2,65536]{2,1,0:T(2,128)(2,1)S(1)}, u32[]{:S(2)}) copy-start(bf16[3,2,65536]{2,1,0:T(2,128)(2,1)S(1)} %collective-permute-done.15) | copy-start | bytes 2359300
  296.7 124.5 %collective-permute-start.6 = (bf16[3,2,65536]{2,1,0:T(2,128)(2,1)S(1)}, bf16[3,2,65536]{2,1,0:T(2,128)(2,1)S(1)}, u32[]{:S(2)}, u32[]{:S(2)}) collective-permute-start(bf16[3,2,65536]{2,1,0:T(2,128)(2,1)S(1)} %reshape.51), channel_id=1, source_target_pairs={{0,4},{1,5},{2,6},{3,7},{4,8},{5,9},{6,10},{7,11},{8,12},{9,13},{1... | collective-permute-start | bytes 2359304 | tf_op jit(solution)/shard_map/ppermute | solution.py:31
  341.7 75.0 %copy-start.7 = (bf16[3,2,65536]{2,1,0:T(2,128)(2,1)}, bf16[3,2,65536]{2,1,0:T(2,128)(2,1)S(1)}, u32[]{:S(2)}) copy-start(bf16[3,2,65536]{2,1,0:T(2,128)(2,1)S(1)} %collective-permute-done.16) | copy-start | bytes 2359300
  341.7 105.0 %collective-permute-start.7 = (bf16[3,2,65536]{2,1,0:T(2,128)(2,1)S(1)}, bf16[3,2,65536]{2,1,0:T(2,128)(2,1)S(1)}, u32[]{:S(2)}, u32[]{:S(2)}) collective-permute-start(bf16[3,2,65536]{2,1,0:T(2,128)(2,1)S(1)} %reshape.51), channel_id=1, source_target_pairs={{0,3},{1,4},{2,5},{3,6},{4,7},{5,8},{6,9},{7,10},{8,11},{9,12},{10... | collective-permute-start | bytes 2359304 | tf_op jit(solution)/shard_map/ppermute | solution.py:31
  380.6 36.1 %copy-start.8 = (bf16[3,2,65536]{2,1,0:T(2,128)(2,1)}, bf16[3,2,65536]{2,1,0:T(2,128)(2,1)S(1)}, u32[]{:S(2)}) copy-start(bf16[3,2,65536]{2,1,0:T(2,128)(2,1)S(1)} %collective-permute-done.3) | copy-start | bytes 2359300
  380.6 83.0 %collective-permute-start.8 = (bf16[3,2,65536]{2,1,0:T(2,128)(2,1)S(1)}, bf16[3,2,65536]{2,1,0:T(2,128)(2,1)S(1)}, u32[]{:S(2)}, u32[]{:S(2)}) collective-permute-start(bf16[3,2,65536]{2,1,0:T(2,128)(2,1)S(1)} %reshape.51), channel_id=1, source_target_pairs={{0,2},{1,3},{2,4},{3,5},{4,6},{5,7},{6,8},{7,9},{8,10},{9,11},{10,... | collective-permute-start | bytes 2359304 | tf_op jit(solution)/shard_map/ppermute | solution.py:31
  416.7 0.9 copy-start.9
  417.6 46.9 %collective-permute-start.9 = (bf16[3,2,65536]{2,1,0:T(2,128)(2,1)S(1)}, bf16[3,2,65536]{2,1,0:T(2,128)(2,1)}, u32[]{:S(2)}, u32[]{:S(2)}) collective-permute-start(bf16[3,2,65536]{2,1,0:T(2,128)(2,1)S(1)} %reshape.51), channel_id=1, source_target_pairs={{0,1},{1,2},{2,3},{3,4},{4,5},{5,6},{6,7},{7,8},{8,9},{9,10},{10,1... | collective-permute-start | bytes 2359304 | tf_op jit(solution)/shard_map/ppermute | solution.py:31
  421.2 42.4 %copy-start.10 = (bf16[3,2,65536]{2,1,0:T(2,128)(2,1)}, bf16[3,2,65536]{2,1,0:T(2,128)(2,1)S(1)}, u32[]{:S(2)}) copy-start(bf16[3,2,65536]{2,1,0:T(2,128)(2,1)S(1)} %collective-permute-done.5) | copy-start | bytes 2359300
  421.2 42.4 %copy-start.11 = (bf16[3,2,65536]{2,1,0:T(2,128)(2,1)}, bf16[3,2,65536]{2,1,0:T(2,128)(2,1)S(1)}, u32[]{:S(2)}) copy-start(bf16[3,2,65536]{2,1,0:T(2,128)(2,1)S(1)} %collective-permute-done.6) | copy-start | bytes 2359300
  446.7 16.9 %copy-start.12 = (bf16[3,2,65536]{2,1,0:T(2,128)(2,1)}, bf16[3,2,65536]{2,1,0:T(2,128)(2,1)S(1)}, u32[]{:S(2)}) copy-start(bf16[3,2,65536]{2,1,0:T(2,128)(2,1)S(1)} %collective-permute-done.7) | copy-start | bytes 2359300
  463.6 0.9 copy-start.13
  682.7 1.4 copy-start.1
Sparse Core Ops, SparseCore 0:
  685.2 86.6 reduce-scatter.1
where the time goes:
time: 793 us; the launch traced here: 779 us
  starting transfers between devices  318 us (40%)
  local copies, waits for them, and re-layouts  218 us (27%)
  waiting for transfers between devices  199 us (25%)
  other arithmetic  22 us (3%)
  between operations  15.2 us (2%)
    ppermute x16, starting transfers between devices, from_behind(): lax.ppermute(value, axis, [(source, source + steps) for source in range(f...  312 us
    concatenate x1, local copies, waits for them, and re-layouts, per_device(): stacked = jnp.concatenate(below + [along_y] + above, axis=1)  211 us
    ppermute x16, waiting for transfers between devices, from_behind(): lax.ppermute(value, axis, [(source, source + steps) for source in range(f...  107 us
    reduce_scatter x1, waiting for transfers between devices, per_device(): lax.psum_scatter(partial_sum, 'subj', scatter_dimension=1, tiled=True)  86.1 us
    add x1, other arithmetic, transport(): pulled = pulled + weights_z[index_z] * plane_sum  16.3 us
  transfers between devices with their start and end apart: 19, of which 9 were waited for; matrix products, arithmetic and copies ran while one was open for 0% of the time, Pallas kernels for 0%

commit v1 on v0

--- a/solution.py
+++ b/solution.py
@@ -23,12 +23,6 @@
             axis=dim,
         )
     return cells
-
-
-def from_behind(value, axis, steps):
-    count = lax.axis_size(axis)
-    first, last = (max(0, -steps), min(count, count - steps))
-    return lax.ppermute(value, axis, [(source, source + steps) for source in range(first, last)])
 
 
 def taps_matrix(rows, cols, offset):
@@ -89,25 +83,27 @@
     along_x = along_x.astype(jnp.bfloat16).reshape(subjects * 3, depth, height, breadth)
     along_y = jnp.einsum("mznx,ny->mzyx", along_x, kernel_y, preferred_element_type=jnp.float32)
     along_y = along_y.astype(jnp.bfloat16).reshape(subjects * 3, depth, height * breadth)
-    reach = (14 + depth) // depth
-    below = []
-    for distance in range(reach, 0, -1):
-        start = max(0, distance * depth - 15)
-        below.append(from_behind(along_y[:, start:], "slab", distance))
-    above = []
-    for distance in range(1, reach + 1):
-        count = min(depth, 15 - (distance - 1) * depth)
-        above.append(from_behind(along_y[:, :count], "slab", -distance))
-    stacked = jnp.concatenate(below + [along_y] + above, axis=1)
-    kernel_z = taps_matrix(depth + 30, depth, 15)
-    velocity = jnp.einsum(
-        "mlq,lz->mzq", stacked, kernel_z, preferred_element_type=jnp.float32
-    ).astype(jnp.bfloat16)
+    count = lax.axis_size("slab")
+    blocks = along_y.reshape(3, depth, count, height * breadth // count)
+    gathered = lax.all_to_all(
+        blocks.transpose(2, 1, 0, 3), "slab", split_axis=0, concat_axis=0, tiled=True
+    )
+    planes = gathered.reshape(count * depth, 3 * (height * breadth // count))
+    kernel_z = taps_matrix(count * depth, count * depth, 0)
+    smooth = jnp.dot(kernel_z, planes, preferred_element_type=jnp.float32).astype(jnp.bfloat16)
+    returned = lax.all_to_all(
+        smooth.reshape(count, depth, 3, -1), "slab", split_axis=0, concat_axis=0, tiled=True
+    )
+    velocity = returned.transpose(2, 1, 0, 3)
     velocity = velocity.reshape(subjects, 3, depth, height, breadth)
     product = jnp.sum(gradient[None] * velocity.astype(jnp.float32), axis=1)
     alignment = product.astype(jnp.bfloat16)
     partial_sum = jnp.sum(pulled * (1.0 + product), axis=0)
-    template_update = lax.psum_scatter(partial_sum, "subj", scatter_dimension=1, tiled=True)
+    shares = lax.axis_size("subj")
+    parts = partial_sum.reshape(depth, shares, height // shares, breadth).transpose(1, 0, 2, 3)
+    template_update = jnp.sum(
+        lax.all_to_all(parts, "subj", split_axis=0, concat_axis=0, tiled=True), axis=0
+    )
     return (alignment, template_update)
 
 

time: 793 us -> 126 us (0.16); the launches traced: 779 us -> 126 us
  starting transfers between devices: 318 us -> 13.2 us
  local copies, waits for them, and re-layouts: 218 us -> 5.86 us
  waiting for transfers between devices: 199 us -> 18.2 us
  blocking collectives: 0 us -> 63.4 us
  between operations: 15.2 us -> 1.54 us
    ppermute x16 -> x0, starting transfers between devices: 312 us -> none  [from_behind(): lax.ppermute(value, axis, [(source, source + steps) for source in range(f...]
    concatenate x1 -> x0, local copies, waits for them, and re-layouts: 211 us -> none  [per_device(): stacked = jnp.concatenate(below + [along_y] + above, axis=1)]
    ppermute x16 -> x0, waiting for transfers between devices: 107 us -> none  [from_behind(): lax.ppermute(value, axis, [(source, source + steps) for source in range(f...]
    reduce_scatter x1 -> x0, waiting for transfers between devices: 86.1 us -> none  [per_device(): lax.psum_scatter(partial_sum, 'subj', scatter_dimension=1, tiled=True)]
    all_to_all x0 -> x2, blocking collectives: none -> 63.4 us  [the longest x1 34.8 us: per_device(): lax.all_to_all(blocks.transpose(2, 1, 0, 3), 'slab', split_axis=0, concat...]
    all_to_all x0 -> x1, waiting for transfers between devices: none -> 8.62 us  [per_device(): lax.all_to_all(parts, 'subj', split_axis=0, concat_axis=0, tiled=True)]
  transfers between devices with their start and end apart: 19 -> 3, of which waited for: 9 -> 3; matrix products, arithmetic and copies ran while one was open for 0% -> 1% of each run, Pallas kernels for 0% -> 0%
where the time goes in v1:
time: 126 us
  blocking collectives  63.4 us (50%)
  other arithmetic  22.4 us (18%)
  waiting for transfers between devices  18.2 us (14%)
  starting transfers between devices  13.2 us (10%)
  local copies, waits for them, and re-layouts  5.86 us (5%)
  between operations  1.54 us (1%)
    all_to_all x1, blocking collectives, per_device(): lax.all_to_all(blocks.transpose(2, 1, 0, 3), 'slab', split_axis=0, concat...  34.8 us
    all_to_all x1, blocking collectives, per_device(): lax.all_to_all(smooth.reshape(count, depth, 3, -1), 'slab', split_axis=0,...  28.6 us
    add x1, other arithmetic, transport(): pulled = pulled + weights_z[index_z] * plane_sum  16.3 us
    ppermute x1, waiting for transfers between devices, padded(): lax.ppermute(tail, axis, [(i, (i + 1) % count) for i in range(ends)])  8.88 us
    all_to_all x1, waiting for transfers between devices, per_device(): lax.all_to_all(parts, 'subj', split_axis=0, concat_axis=0, tiled=True)  8.62 us
    all_to_all x1, starting transfers between devices, per_device(): lax.all_to_all(parts, 'subj', split_axis=0, concat_axis=0, tiled=True)  7.07 us
    ppermute x1, starting transfers between devices, padded(): lax.ppermute(tail, axis, [(i, (i + 1) % count) for i in range(ends)])  4.67 us
  transfers between devices with their start and end apart: 3, of which 3 were waited for; matrix products, arithmetic and copies ran while one was open for 1% of the time, Pallas kernels for 0%

profile of v1, /device:TPU:1, one launch (start us, length us, event | category | flops | bytes accessed | tf_op | source)
XLA Modules:
  0.0 125.7 jit_solution(3954586996020017625)
XLA Ops:
  0.6 0.0 copy-start.3
  0.6 0.0 copy-start.5
  0.7 1.4 %collective-permute-start.1 = (bf16[1,2,256,256]{3,2,1,0:T(8,128)(2,1)}, bf16[1,2,256,256]{3,2,1,0:T(8,128)(2,1)S(1)}, u32[]{:S(2)}, u32[]{:S(2)}) collective-permute-start(bf16[1,2,256,256]{3,2,1,0:T(8,128)(2,1)} %param.5), channel_id=1, source_target_pairs={{1,0},{2,1},{3,2},{4,3},{5,4},{6,5},{7,6},{8,7},{9,8},{10,9},{11,1... | collective-permute-start | bytes 786440 | tf_op jit(solution)/shard_map/ppermute | solution.py:21
  2.1 4.7 %collective-permute-start = (bf16[1,2,256,256]{3,2,1,0:T(8,128)(2,1)}, bf16[1,2,256,256]{3,2,1,0:T(8,128)(2,1)S(1)}, u32[]{:S(2)}, u32[]{:S(2)}) collective-permute-start(bf16[1,2,256,256]{3,2,1,0:T(8,128)(2,1)} %param.5), channel_id=1, source_target_pairs={{0,1},{1,2},{2,3},{3,4},{4,5},{5,6},{6,7},{7,8},{8,9},{9,10},{10,1... | collective-permute-start | bytes 786440 | tf_op jit(solution)/shard_map/ppermute | solution.py:19
  6.8 0.6 exponential_reduce_fusion
  8.1 0.7 collective-permute-done.1
  8.8 8.9 %collective-permute-done = bf16[1,2,256,256]{3,2,1,0:T(8,128)(2,1)S(1)} collective-permute-done((bf16[1,2,256,256]{3,2,1,0:T(8,128)(2,1)}, bf16[1,2,256,256]{3,2,1,0:T(8,128)(2,1)S(1)}, u32[]{:S(2)}, u32[]{:S(2)}) %collective-permute-start) | collective-permute-done | bytes 262176 | tf_op jit(solution)/shard_map/ppermute | solution.py:19
  17.7 1.8 %select_maximum_fusion = bf16[1,6,260,260]{3,2,1,0:T(8,128)(2,1)S(1)} fusion(bf16[1,2,256,256]{3,2,1,0:T(8,128)(2,1)S(1)} %collective-permute-done.1, bf16[1,2,256,256]{3,2,1,0:T(8,128)(2,1)} %param.5, bf16[1,2,256,256]{3,2,1,0:T(8,128)(2,1)S(1)} %collective-permute-done), kind=kLoop, calls=%fused_computation.18 | loop fusion | flops 7706400 | bytes 1597632 | tf_op jit(solution)/shard_map/concatenate | solution.py:17
  19.5 0.0 copy-done.3
  19.5 0.0 copy-done.5
  19.5 0.0 copy-start.2
  19.5 0.0 copy-start.4
  19.5 16.3 %multiply_add_fusion = f32[1,2,256,256]{3,2,1,0:T(8,128)S(1)} fusion(bf16[1,2,256,256]{3,2,1,0:T(8,128)(2,1)S(1)} %collective-permute-done.1, bf16[1,2,256,256]{3,2,1,0:T(8,128)(2,1)S(1)} %copy-done.3, bf16[1,2,256,256]{3,2,1,0:T(8,128)(2,1)S(1)} %collective-permute-done, s32[1,2,256,256]{3,2,1,0:T(8,128)S(1)} %copy-done.5, ...), kind=kLoop, calls=%fused_computation.56 | loop fusion | flops 77463552 | bytes 33292288 | tf_op jit(solution)/shard_map/vmap()/add | solution.py:69
  35.8 0.0 copy-start
  35.8 0.0 copy-done.2
  35.8 0.0 copy-done.4
  35.8 0.3 fusion.5
  36.1 0.4 convolution_convert_fusion.1
  36.5 0.1 copy-done
  36.5 0.4 fusion.7
  36.9 0.5 reshape_reshape.3
  37.4 0.8 copy.22
  38.2 34.8 %all_to_all.15 = bf16[64,2,3,1024]{3,1,2,0:T(2,128)(2,1)S(1)} all-to-all(bf16[64,2,3,1024]{3,1,2,0:T(2,128)(2,1)S(1)} %bitcast.41), channel_id=1, replica_groups=mesh['subj'=4,'slab'=64] {'slab'}, dimensions={0} | all-to-all | bytes 1572864 | tf_op jit(solution)/shard_map/all_to_all | solution.py:88
  73.1 0.5 copy.15
  73.6 0.4 copy.20
  74.0 0.4 convolution_convert_fusion
  74.3 1.2 reshape.54
  75.5 0.7 copy.16
  76.2 28.6 %all_to_all.16 = bf16[64,2,3,1024]{3,1,2,0:T(2,128)(2,1)S(1)} all-to-all(bf16[64,2,3,1024]{3,1,2,0:T(2,128)(2,1)S(1)} %copy.16), channel_id=1, replica_groups=mesh['subj'=4,'slab'=64] {'slab'}, dimensions={0} | all-to-all | bytes 1572864 | tf_op jit(solution)/shard_map/all_to_all | solution.py:94
  104.7 0.5 convert_bitcast_fusion
  105.3 0.5 copy.17
  105.8 0.4 reshape.56
  106.2 0.0 copy-start.1
  106.3 1.4 %fusion.6 = f32[2,256,256]{2,1,0:T(8,128)S(1)} fusion(f32[3,2,256,256]{3,2,1,0:T(8,128)S(1)} %reshape.56, bf16[3,2,256,256]{3,2,1,0:T(8,128)(2,1)} %param.7), kind=kLoop, calls=%fused_computation.14 | loop fusion | flops 1048576 | bytes 2883584 | tf_op jit(solution)/shard_map/reduce_sum | solution.py:99
  107.7 0.0 copy-done.1
  107.7 0.1 bitcast_multiply_fusion
  107.8 0.8 copy.18
  108.6 7.1 %all-to-all-start.2 = ((f32[4,2,64,256]{3,2,1,0:T(8,128)}), f32[4,2,64,256]{3,2,1,0:T(8,128)S(1)}, u32[]{:S(2)}, u32[]{:S(2)}) async-start(f32[4,2,64,256]{3,2,1,0:T(8,128)} %copy.18), calls=%async_computation.2 | async-start | bytes 1048576 | tf_op jit(solution)/shard_map/all_to_all | solution.py:105
  115.7 0.7 convert_bitcast_fusion.1
  116.4 8.6 %all-to-all-done.2 = f32[4,2,64,256]{3,2,1,0:T(8,128)S(1)} async-done(((f32[4,2,64,256]{3,2,1,0:T(8,128)}), f32[4,2,64,256]{3,2,1,0:T(8,128)S(1)}, u32[]{:S(2)}, u32[]{:S(2)}) %all-to-all-start.2) | async-done | bytes 524320 | tf_op jit(solution)/shard_map/all_to_all | solution.py:105
  125.0 0.7 reduce_sum.29
Async XLA Ops:
  0.6 18.8 %copy-start.3 = (bf16[1,2,256,256]{3,2,1,0:T(8,128)(2,1)S(1)}, bf16[1,2,256,256]{3,2,1,0:T(8,128)(2,1)}, u32[]{:S(2)}) copy-start(bf16[1,2,256,256]{3,2,1,0:T(8,128)(2,1)} %param.5) | copy-start | bytes 786436
  0.6 18.8 %copy-start.5 = (s32[1,2,256,256]{3,2,1,0:T(8,128)S(1)}, s32[1,2,256,256]{3,2,1,0:T(8,128)}, u32[]{:S(2)}) copy-start(s32[1,2,256,256]{3,2,1,0:T(8,128)} %param.6) | copy-start | bytes 1572868
  0.7 8.1 %collective-permute-start.1 = (bf16[1,2,256,256]{3,2,1,0:T(8,128)(2,1)}, bf16[1,2,256,256]{3,2,1,0:T(8,128)(2,1)S(1)}, u32[]{:S(2)}, u32[]{:S(2)}) collective-permute-start(bf16[1,2,256,256]{3,2,1,0:T(8,128)(2,1)} %param.5), channel_id=1, source_target_pairs={{1,0},{2,1},{3,2},{4,3},{5,4},{6,5},{7,6},{8,7},{9,8},{10,9},{11,1... | collective-permute-start | bytes 786440 | tf_op jit(solution)/shard_map/ppermute | solution.py:21
  2.1 15.6 %collective-permute-start = (bf16[1,2,256,256]{3,2,1,0:T(8,128)(2,1)}, bf16[1,2,256,256]{3,2,1,0:T(8,128)(2,1)S(1)}, u32[]{:S(2)}, u32[]{:S(2)}) collective-permute-start(bf16[1,2,256,256]{3,2,1,0:T(8,128)(2,1)} %param.5), channel_id=1, source_target_pairs={{0,1},{1,2},{2,3},{3,4},{4,5},{5,6},{6,7},{7,8},{8,9},{9,10},{10,1... | collective-permute-start | bytes 786440 | tf_op jit(solution)/shard_map/ppermute | solution.py:19
  19.5 16.3 %copy-start.2 = (bf16[3,2,256,256]{3,2,1,0:T(8,128)(2,1)S(1)}, bf16[3,2,256,256]{3,2,1,0:T(8,128)(2,1)}, u32[]{:S(2)}) copy-start(bf16[3,2,256,256]{3,2,1,0:T(8,128)(2,1)} %param.7) | copy-start | bytes 2359300
  19.5 16.3 %copy-start.4 = (bf16[1,3,2,256,256]{4,3,2,1,0:T(8,128)(2,1)S(1)}, bf16[1,3,2,256,256]{4,3,2,1,0:T(8,128)(2,1)}, u32[]{:S(2)}) copy-start(bf16[1,3,2,256,256]{4,3,2,1,0:T(8,128)(2,1)} %param.4) | copy-start | bytes 2359300
  35.8 0.8 copy-start
  106.2 1.4 %copy-start.1 = (f32[1,2,256,256]{3,2,1,0:T(8,128)S(1)}, f32[1,2,256,256]{3,2,1,0:T(8,128)}, u32[]{:S(2)}) copy-start(f32[1,2,256,256]{3,2,1,0:T(8,128)} %copy-done) | copy-start | bytes 1572868
  108.6 16.4 %all-to-all-start.2 = ((f32[4,2,64,256]{3,2,1,0:T(8,128)}), f32[4,2,64,256]{3,2,1,0:T(8,128)S(1)}, u32[]{:S(2)}, u32[]{:S(2)}) async-start(f32[4,2,64,256]{3,2,1,0:T(8,128)} %copy.18), calls=%async_computation.2 | async-start | bytes 1048576 | tf_op jit(solution)/shard_map/all_to_all | solution.py:105

commit v2 on v1

v2 whole, which is shorter than its diff:
```python
import math

import jax
import jax.numpy as jnp
from jax import lax
from jax.experimental import pallas as pl
from jax.experimental.pallas import tpu as pltpu
from jax.sharding import PartitionSpec as P

rim = 2
bias = 8
decay = 8.0
reach = 15
taps = 2 * rim + 1
lanes = 128
rows = 8
MESH = pl.DeviceIdType.MESH
scale = math.sqrt(sum(math.exp(-2.0 * abs(t) / decay) for t in range(-reach, reach + 1)))
ratio = math.exp(-1.0 / decay)


def band(size):
    lag = jnp.abs(
        lax.broadcasted_iota(jnp.int32, (size, size), 0)
        - lax.broadcasted_iota(jnp.int32, (size, size), 1)
    )
    values = jnp.exp(lag.astype(jnp.float32) * (-1.0 / decay)) / scale
    return jnp.where(lag <= reach, values, 0.0).astype(jnp.bfloat16)


def axis_weights(digit):
    place = digit.astype(jnp.float32) * 0.25 - bias * 0.25
    return [jnp.maximum(1.0 - jnp.abs(place - offset), 0.0) for offset in range(-rim, rim + 1)]


def drain(ref, sem):
    pltpu.make_async_copy(ref, ref, sem).wait()


def kernel(
    count,
    momentum,
    adjoint,
    code,
    gradient,
    alignment,
    update,
    frame,
    shifted,
    codes,
    moments,
    grads,
    pulled,
    kern,
    outgoing,
    incoming,
    far_grads,
    forward,
    backward,
    products,
    returned,
    shares,
    others,
    local_sem,
    halo_send,
    halo_recv,
    grad_send,
    grad_recv,
    swap_send,
    swap_recv,
    out_send,
    in_recv,
    back_send,
    back_recv,
    share_send,
    share_recv,
):
    subject = lax.axis_index("subj")
    slab = lax.axis_index("slab")
    subjects = others.shape[0] + 1
    components, depth, height, breadth = grads.shape
    halves = breadth // lanes
    blocks = height // rows
    partner = subject + 1 - 2 * (subject % 2)
    mine = subject % 2

    def slab_peer(step):
        hop = (step + 1) // 2
        return lax.rem(slab + count + jnp.where(step % 2 == 1, hop, -hop), count)

    barrier = pltpu.get_barrier_semaphore()

    def greet(step, carry):
        pl.semaphore_signal(
            barrier, inc=1, device_id=(subject, slab_peer(step)), device_id_type=MESH
        )
        return carry

    loads = [
        pltpu.make_async_copy(adjoint.at[0], frame.at[pl.ds(2, 2)], local_sem.at[0]),
        pltpu.make_async_copy(code.at[0], codes, local_sem.at[1]),
        pltpu.make_async_copy(momentum.at[0], moments, local_sem.at[2]),
        pltpu.make_async_copy(gradient, grads, local_sem.at[3]),
    ]
    for load in loads:
        load.start()
    lax.fori_loop(1, count, greet, 0)
    for step in range(1, subjects):
        pl.semaphore_signal(
            barrier,
            inc=1,
            device_id=(lax.rem(subject + step, subjects), slab),
            device_id_type=MESH,
        )
    kern[...] = band(max(breadth, height))
    shifted[:, :, :, pl.ds(0, rows), :] = jnp.zeros((6, taps, halves, rows, lanes), jnp.float32)
    shifted[:, :, :, pl.ds(rows + height, rows), :] = jnp.zeros(
        (6, taps, halves, rows, lanes), jnp.float32
    )
    column = lax.broadcasted_iota(jnp.int32, (height, breadth), 1)

    def spread(plane):
        values = frame[plane].astype(jnp.float32)
        for index in range(taps):
            move = index - rim
            if move == 0:
                seen = values
            else:
                turned = pltpu.roll(values, (-move) % breadth, 1)
                inside = (column + move >= 0) & (column + move < breadth)
                seen = jnp.where(inside, turned, 0.0)
            for half in range(halves):
                shifted[plane, index, half, pl.ds(rows, height), :] = seen[
                    :, half * lanes : (half + 1) * lanes
                ]

    loads[0].wait()
    pl.semaphore_wait(barrier, count - 1 + subjects - 1)

    up = pltpu.make_async_remote_copy(
        src_ref=adjoint.at[0],
        dst_ref=frame.at[pl.ds(0, 2)],
        send_sem=halo_send.at[0],
        recv_sem=halo_recv.at[0],
        device_id=(subject, lax.rem(slab + 1, count)),
        device_id_type=MESH,
    )
    down = pltpu.make_async_remote_copy(
        src_ref=adjoint.at[0],
        dst_ref=frame.at[pl.ds(4, 2)],
        send_sem=halo_send.at[1],
        recv_sem=halo_recv.at[1],
        device_id=(subject, lax.rem(slab + count - 1, count)),
        device_id_type=MESH,
    )

    up.start()
    down.start()

    def area(peer):
        return (
            pl.ds(pl.multiple_of((peer // halves) * rows, rows), rows),
            pl.ds(pl.multiple_of((peer % halves) * lanes, lanes), lanes),
        )

    def send_grad(step, carry):
        peer = slab_peer(step)
        row, col = area(peer)
        pltpu.make_async_remote_copy(
            src_ref=gradient.at[:, mine, row, col],
            dst_ref=far_grads.at[mine, slab],
            send_sem=grad_send,
            recv_sem=grad_recv,
            device_id=(subject, peer),
            device_id_type=MESH,
        ).start()
        return carry

    lax.fori_loop(1, count, send_grad, 0)
    row, col = area(slab)
    pltpu.make_async_copy(
        gradient.at[:, mine, row, col], far_grads.at[mine, slab], grad_recv
    ).start()

    spread(2)
    spread(3)
    for load in loads[1:]:
        load.wait()
    up.wait()
    down.wait()

    @pl.when(slab == 0)
    def _():
        frame[pl.ds(0, 2)] = jnp.zeros((2, height, breadth), jnp.bfloat16)

    @pl.when(slab == count - 1)
    def _():
        frame[pl.ds(4, 2)] = jnp.zeros((2, height, breadth), jnp.bfloat16)

    for plane in (0, 1, 4, 5):
        spread(plane)

    for plane in range(depth):

        def transport(block, carry):
            start = pl.multiple_of(block * rows, rows)
            for half in range(halves):
                cell = codes[plane, pl.ds(start, rows), pl.ds(half * lanes, lanes)]
                weights_z = axis_weights(cell // 256)
                weights_y = axis_weights(cell // 16 % 16)
                weights_x = axis_weights(cell % 16)
                total = None
                for index_z in range(taps):
                    plane_sum = None
                    for index_y in range(taps):
                        row_sum = None
                        for index_x in range(taps):
                            term = weights_x[index_x] * shifted[
                                plane + index_z,
                                index_x,
                                half,
                                pl.ds(start + (rows - rim + index_y), rows),
                                :,
                            ]
                            row_sum = term if row_sum is None else row_sum + term
                        term = weights_y[index_y] * row_sum
                        plane_sum = term if plane_sum is None else plane_sum + term
                    term = weights_z[index_z] * plane_sum
                    total = term if total is None else total + term
                pulled[plane, pl.ds(start, rows), pl.ds(half * lanes, lanes)] = total
            return carry

        lax.fori_loop(0, blocks, transport, 0)
        for part in range(components):
            mixed = moments[part, plane].astype(jnp.float32) + pulled[plane] * grads[
                part, plane
            ].astype(jnp.float32)
            along_x = jnp.dot(
                mixed.astype(jnp.bfloat16), kern[...], preferred_element_type=jnp.float32
            )
            along_y = jnp.dot(
                kern[:height, :height], along_x.astype(jnp.bfloat16), preferred_element_type=jnp.float32
            ).astype(jnp.bfloat16)
            for half in range(halves):
                outgoing[plane, :, half, part] = along_y[
                    :, half * lanes : (half + 1) * lanes
                ].reshape(blocks, rows, lanes)

        def send(step, carry):
            peer = slab_peer(step)
            pltpu.make_async_remote_copy(
                src_ref=outgoing.at[plane, peer // halves, peer % halves],
                dst_ref=incoming.at[plane, slab],
                send_sem=out_send.at[plane],
                recv_sem=in_recv.at[plane],
                device_id=(subject, peer),
                device_id_type=MESH,
            ).start()
            return carry

        lax.fori_loop(1, count, send, 0)
        pltpu.make_async_copy(
            outgoing.at[plane, slab // halves, slab % halves],
            incoming.at[plane, slab],
            in_recv.at[plane],
        ).start()

    drain(far_grads.at[mine], grad_recv)
    swap = pltpu.make_async_remote_copy(
        src_ref=far_grads.at[mine],
        dst_ref=far_grads.at[mine],
        send_sem=swap_send,
        recv_sem=swap_recv,
        device_id=(partner, slab),
        device_id_type=MESH,
    )
    swap.start()
    swap.wait()
    for plane in range(depth):
        drain(incoming.at[plane], in_recv.at[plane])

    gone = ratio ** (reach + 1)
    last = count - 1
    zero = jnp.zeros((components, rows, lanes), jnp.float32)
    window = (reach + 1) // depth

    def field(plane, index):
        return incoming[plane, index].astype(jnp.float32)

    def advance(with_tail):
        def step(index, carry):
            ahead, behind = carry
            mirror = last - index
            for plane in range(depth):
                ahead = ahead * ratio + field(plane, index)
                if with_tail:
                    ahead = ahead - gone * field(plane, index - window)
                forward[index, plane] = ahead
            for plane in reversed(range(depth)):
                here = field(plane, mirror)
                behind = behind * ratio + here
                if with_tail:
                    behind = behind - gone * field(plane, mirror + window)
                backward[mirror, plane] = behind - here
            return ahead, behind

        return step

    edge = min(window, count)
    carry = lax.fori_loop(0, edge, advance(False), (zero, zero))
    lax.fori_loop(edge, count, advance(True), carry)

    def combine(index, carry):
        for plane in range(depth):
            velocity = (forward[index, plane] + backward[index, plane]) * (1.0 / scale)
            slope = far_grads[plane, index].astype(jnp.float32)
            products[index, plane] = jnp.sum(slope * velocity, axis=0).astype(jnp.bfloat16)
        return carry

    lax.fori_loop(0, count, combine, 0)

    def send_back(step, carry):
        peer = slab_peer(step)
        pltpu.make_async_remote_copy(
            src_ref=products.at[peer],
            dst_ref=returned.at[slab // halves, slab % halves],
            send_sem=back_send,
            recv_sem=back_recv,
            device_id=(subject, peer),
            device_id_type=MESH,
        ).start()
        return carry

    lax.fori_loop(1, count, send_back, 0)
    pltpu.make_async_copy(
        products.at[slab], returned.at[slab // halves, slab % halves], back_recv
    ).start()
    drain(returned, back_recv)

    part_rows = height // subjects
    part_blocks = blocks // subjects

    def partial(owner, plane, half):
        block = owner * part_blocks
        values = returned[pl.ds(block, part_blocks), half, plane]
        values = values.reshape(part_rows, lanes).astype(jnp.float32)
        start = pl.multiple_of(owner * part_rows, part_rows)
        moved = pulled[plane, pl.ds(start, part_rows), pl.ds(half * lanes, lanes)]
        return moved * (1.0 + values)

    share_copies = []
    for step in range(1, subjects):
        owner = lax.rem(subject + step, subjects)
        for plane in range(depth):
            for half in range(halves):
                shares[step - 1, plane, :, pl.ds(half * lanes, lanes)] = partial(
                    owner, plane, half
                ).astype(jnp.bfloat16)
        copy = pltpu.make_async_remote_copy(
            src_ref=shares.at[step - 1],
            dst_ref=others.at[step - 1],
            send_sem=share_send.at[step - 1],
            recv_sem=share_recv.at[step - 1],
            device_id=(owner, slab),
            device_id_type=MESH,
        )
        copy.start()
        share_copies.append(copy)
    for plane in range(depth):
        for half in range(halves):
            alignment[0, plane, :, pl.ds(half * lanes, lanes)] = returned[:, half, plane].reshape(
                height, lanes
            )
    for copy in share_copies:
        copy.wait()
    for plane in range(depth):
        for half in range(halves):
            total = partial(subject, plane, half)
            for step in range(1, subjects):
                total = total + others[
                    step - 1, plane, :, pl.ds(half * lanes, lanes)
                ].astype(jnp.float32)
            update[plane, :, pl.ds(half * lanes, lanes)] = total

    sent = pl.ds(0, count - 1)
    drain(far_grads.at[0, sent], grad_send)
    for plane in range(depth):
        drain(incoming.at[0, sent], out_send.at[plane])
    drain(products.at[sent], back_send)


def solution(mesh):
    count = mesh.shape["slab"]
    subjects = mesh.shape["subj"]

    def per_device(momentum, adjoint, code, gradient):
        components, depth, height, breadth = gradient.shape
        halves = breadth // lanes
        blocks = height // rows
        part = height // subjects
        vmem, dma = pltpu.VMEM, pltpu.SemaphoreType.DMA
        half, full = jnp.bfloat16, jnp.float32

        def body(*refs):
            kernel(count, *refs)

        return pl.pallas_call(
            body,
            out_shape=(
                jax.ShapeDtypeStruct((1, depth, height, breadth), half),
                jax.ShapeDtypeStruct((depth, part, breadth), full),
            ),
            in_specs=[pl.BlockSpec(memory_space=pl.ANY)] * 4,
            out_specs=(pl.BlockSpec(memory_space=vmem), pl.BlockSpec(memory_space=vmem)),
            scratch_shapes=[
                vmem((6, height, breadth), half),
                vmem((6, taps, halves, height + 2 * rows, lanes), full),
                vmem((depth, height, breadth), jnp.int32),
                vmem((components, depth, height, breadth), half),
                vmem((components, depth, height, breadth), half),
                vmem((depth, height, breadth), full),
                vmem((breadth, breadth), half),
                vmem((depth, blocks, halves, components, rows, lanes), half),
                vmem((depth, count, components, rows, lanes), half),
                vmem((2, count, components, rows, lanes), half),
                vmem((count, depth, components, rows, lanes), full),
                vmem((count, depth, components, rows, lanes), full),
                vmem((count, depth, rows, lanes), half),
                vmem((blocks, halves, depth, rows, lanes), half),
                vmem((subjects - 1, depth, part, breadth), half),
                vmem((subjects - 1, depth, part, breadth), half),
                dma((4,)),
                dma((2,)),
                dma((2,)),
                dma,
                dma,
                dma,
                dma,
                dma((2,)),
                dma((2,)),
                dma,
                dma,
                dma((subjects - 1,)),
                dma((subjects - 1,)),
            ],
            compiler_params=pltpu.CompilerParams(
                collective_id=0, has_side_effects=True, vmem_limit_bytes=56 * 1024 * 1024
            ),
            name="step",
        )(momentum, adjoint, code, gradient)

    return jax.shard_map(
        per_device,
        mesh=mesh,
        in_specs=(
            P("subj", None, "slab", None, None),
            P("subj", "slab", None, None),
            P("subj", "slab", None, None),
            P(None, "slab", None, None),
        ),
        out_specs=(P("subj", "slab", None, None), P("slab", "subj", None)),
        check_vma=False,
    )
```

time: 126 us -> 77.7 us (0.62)
  Pallas kernels: 0 us -> 74.6 us
  blocking collectives: 63.4 us -> 0 us
  other arithmetic: 22.4 us -> 0 us
  waiting for transfers between devices: 18.2 us -> 0 us
  starting transfers between devices: 13.2 us -> 0 us
  local copies, waits for them, and re-layouts: 5.86 us -> 2.36 us
    pallas_call x0 -> x1, Pallas kernels: none -> 74.6 us  [per_device(): pl.pallas_call(body, out_shape=(jax.ShapeDtypeStruct((1, depth, height, b...]
    all_to_all x2 -> x0, blocking collectives: 63.4 us -> none  [the longest x1 34.8 us: per_device(): lax.all_to_all(blocks.transpose(2, 1, 0, 3), 'slab', split_axis=0, concat...]
    add x1 -> x0, other arithmetic: 16.3 us -> none  [transport(): pulled = pulled + weights_z[index_z] * plane_sum]
    ppermute x2 -> x0, waiting for transfers between devices: 9.59 us -> none  [the longest x1 8.88 us: padded(): lax.ppermute(tail, axis, [(i, (i + 1) % count) for i in range(ends)])]
    all_to_all x1 -> x0, waiting for transfers between devices: 8.62 us -> none  [per_device(): lax.all_to_all(parts, 'subj', split_axis=0, concat_axis=0, tiled=True)]
    all_to_all x1 -> x0, starting transfers between devices: 7.07 us -> none  [per_device(): lax.all_to_all(parts, 'subj', split_axis=0, concat_axis=0, tiled=True)]
    ppermute x2 -> x0, starting transfers between devices: 6.09 us -> none  [the longest x1 4.67 us: padded(): lax.ppermute(tail, axis, [(i, (i + 1) % count) for i in range(ends)])]
    reduce_sum x3 -> x0, other arithmetic: 2.72 us -> none  [the longest x1 1.42 us: per_device(): product = jnp.sum(gradient[None] * velocity.astype(jnp.float32), axis=1)]
  transfers between devices with their start and end apart: 3 -> 0, of which waited for: 3 -> 0; matrix products, arithmetic and copies ran while one was open for 1% -> 0% of each run, Pallas kernels for 0% -> 0%
where the time goes in v2:
time: 77.7 us; the launch traced here: 77.6 us
  Pallas kernels  74.6 us (96%)
  local copies, waits for them, and re-layouts  2.36 us (3%)
    pallas_call x1, Pallas kernels, per_device(): pl.pallas_call(body, out_shape=(jax.ShapeDtypeStruct((1, depth, height, b...  74.6 us
    unnamed x4, local copies, waits for them, and re-layouts  2.36 us

profile of v2, /device:TPU:1, one launch (start us, length us, event | category | flops | bytes accessed | tf_op | source)
XLA Modules:
  0.0 77.6 jit_solution(8898654824646865451)
XLA Ops:
  0.6 74.6 %step.1 = (bf16[1,2,256,256]{3,2,1,0:T(8,128)(2,1)}, f32[2,64,256]{2,1,0:T(8,128)}) custom-call(bf16[1,3,2,256,256]{4,3,2,1,0:T(8,128)(2,1)} %refs_0_.1, bf16[1,2,256,256]{3,2,1,0:T(8,128)(2,1)} %refs_1_.1, s32[1,2,256,256]{3,2,1,0:T(8,128)} %refs_2_.1, bf16[3,2,256,256]{3,2,1,0:T(8,128)(2,1)} %refs_3_.1), custom_call_target="tpu_custom_call" | custom-call | tf_op jit(solution)/shard_map/step/pallas_call | solution.py:407
  75.2 0.0 copy-start
  75.2 1.7 %copy.8 = bf16[1,2,256,256]{3,2,1,0:T(8,128)(2,1)} copy(bf16[1,2,256,256]{3,2,1,0:T(8,128)(2,1)} %get-tuple-element.4) | data formatting | bytes 524288
  76.9 0.0 copy-done
  76.9 0.7 copy.9
Async XLA Ops:
  75.2 1.7 %copy-start = (f32[2,64,256]{2,1,0:T(8,128)S(1)}, f32[2,64,256]{2,1,0:T(8,128)}, u32[]{:S(2)}) copy-start(f32[2,64,256]{2,1,0:T(8,128)} %get-tuple-element.5) | copy-start | bytes 393220

commit v3 on v2

--- a/solution.py
+++ b/solution.py
@@ -28,9 +28,17 @@
     return jnp.where(lag <= reach, values, 0.0).astype(jnp.bfloat16)
 
 
+def position(digit):
+    return digit.astype(jnp.float32) * 0.25 - bias * 0.25
+
+
+def hat(distance):
+    return jnp.maximum(1.0 - jnp.abs(distance), 0.0)
+
+
 def axis_weights(digit):
-    place = digit.astype(jnp.float32) * 0.25 - bias * 0.25
-    return [jnp.maximum(1.0 - jnp.abs(place - offset), 0.0) for offset in range(-rim, rim + 1)]
+    place = position(digit)
+    return [hat(place - offset) for offset in range(-rim, rim + 1)]
 
 
 def drain(ref, sem):
@@ -81,8 +89,11 @@
     components, depth, height, breadth = grads.shape
     halves = breadth // lanes
     blocks = height // rows
+    odd = slab % 2
     partner = subject + 1 - 2 * (subject % 2)
-    mine = subject % 2
+    across = lax.rem(subject + 2, subjects)
+    group_size = count // subjects
+    mine = lax.rem(subject - slab % subjects + subjects, subjects)
 
     def slab_peer(step):
         hop = (step + 1) // 2
@@ -137,25 +148,37 @@
     loads[0].wait()
     pl.semaphore_wait(barrier, count - 1 + subjects - 1)
 
-    up = pltpu.make_async_remote_copy(
-        src_ref=adjoint.at[0],
-        dst_ref=frame.at[pl.ds(0, 2)],
-        send_sem=halo_send.at[0],
-        recv_sem=halo_recv.at[0],
-        device_id=(subject, lax.rem(slab + 1, count)),
-        device_id_type=MESH,
-    )
-    down = pltpu.make_async_remote_copy(
-        src_ref=adjoint.at[0],
-        dst_ref=frame.at[pl.ds(4, 2)],
-        send_sem=halo_send.at[1],
-        recv_sem=halo_recv.at[1],
-        device_id=(subject, lax.rem(slab + count - 1, count)),
-        device_id_type=MESH,
-    )
-
-    up.start()
-    down.start()
+    piece = height // 2
+    near = (5 - 5 * odd, 4 - 3 * odd)
+    far = (1 + 3 * odd, 5 * odd)
+    paired = slab + 1 - 2 * odd
+    onward = lax.rem(slab + 2 - 4 * odd + count, count)
+    direct, passed = [], []
+    for index in range(4):
+        part = pl.ds((index % 2) * piece, piece)
+        plane = odd if index < 2 else 1 - odd
+        direct.append(
+            pltpu.make_async_remote_copy(
+                src_ref=adjoint.at[0, plane, part],
+                dst_ref=frame.at[4 * odd + plane, part],
+                send_sem=halo_send.at[index],
+                recv_sem=halo_recv.at[index],
+                device_id=(subject, paired),
+                device_id_type=MESH,
+            )
+        )
+        passed.append(
+            pltpu.make_async_remote_copy(
+                src_ref=frame.at[near[index // 2], part],
+                dst_ref=frame.at[far[index // 2], part],
+                send_sem=halo_send.at[4 + index],
+                recv_sem=halo_recv.at[4 + index],
+                device_id=(subject, onward),
+                device_id_type=MESH,
+            )
+        )
+    for copy in direct:
+        copy.start()
 
     def area(peer):
         return (
@@ -163,60 +186,52 @@
             pl.ds(pl.multiple_of((peer % halves) * lanes, lanes), lanes),
         )
 
+    own_area = lax.rem(2 * slab, subjects) == subject
+
     def send_grad(step, carry):
-        peer = slab_peer(step)
+        turn = lax.rem(step + slab // subjects, group_size)
+        peer = mine + subjects * turn
         row, col = area(peer)
-        pltpu.make_async_remote_copy(
-            src_ref=gradient.at[:, mine, row, col],
-            dst_ref=far_grads.at[mine, slab],
-            send_sem=grad_send,
-            recv_sem=grad_recv,
-            device_id=(subject, peer),
-            device_id_type=MESH,
-        ).start()
+        source = gradient.at[:, :, row, col]
+        target = far_grads.at[slab % subjects, slab // subjects]
+
+        @pl.when(peer != slab)
+        def _():
+            pltpu.make_async_remote_copy(
+                src_ref=source,
+                dst_ref=target,
+                send_sem=grad_send,
+                recv_sem=grad_recv,
+                device_id=(subject, peer),
+                device_id_type=MESH,
+            ).start()
+
+        @pl.when(peer == slab)
+        def _():
+            pltpu.make_async_copy(source, target, grad_recv).start()
+
         return carry
 
-    lax.fori_loop(1, count, send_grad, 0)
-    row, col = area(slab)
-    pltpu.make_async_copy(
-        gradient.at[:, mine, row, col], far_grads.at[mine, slab], grad_recv
-    ).start()
-
-    spread(2)
-    spread(3)
-    for load in loads[1:]:
-        load.wait()
-    up.wait()
-    down.wait()
-
-    @pl.when(slab == 0)
-    def _():
-        frame[pl.ds(0, 2)] = jnp.zeros((2, height, breadth), jnp.bfloat16)
-
-    @pl.when(slab == count - 1)
-    def _():
-        frame[pl.ds(4, 2)] = jnp.zeros((2, height, breadth), jnp.bfloat16)
-
-    for plane in (0, 1, 4, 5):
-        spread(plane)
-
-    for plane in range(depth):
-
+    lax.fori_loop(0, group_size, send_grad, 0)
+
+    def gather(plane, sources, first):
         def transport(block, carry):
             start = pl.multiple_of(block * rows, rows)
             for half in range(halves):
                 cell = codes[plane, pl.ds(start, rows), pl.ds(half * lanes, lanes)]
-                weights_z = axis_weights(cell // 256)
-                weights_y = axis_weights(cell // 16 % 16)
-                weights_x = axis_weights(cell % 16)
+                place_z = position(lax.shift_right_logical(cell, 8))
+                weights_y = axis_weights(lax.shift_right_logical(cell, 4) & 15)
+                weights_x = axis_weights(cell & 15)
                 total = None
-                for index_z in range(taps):
+                if not first:
+                    total = pulled[plane, pl.ds(start, rows), pl.ds(half * lanes, lanes)]
+                for source in sources:
                     plane_sum = None
                     for index_y in range(taps):
                         row_sum = None
                         for index_x in range(taps):
                             term = weights_x[index_x] * shifted[
-                                plane + index_z,
+                                source,
                                 index_x,
                                 half,
                                 pl.ds(start + (rows - rim + index_y), rows),
@@ -225,12 +240,15 @@
                             row_sum = term if row_sum is None else row_sum + term
                         term = weights_y[index_y] * row_sum
                         plane_sum = term if plane_sum is None else plane_sum + term
-                    term = weights_z[index_z] * plane_sum
+                    offset = jnp.asarray(source - plane - rim, jnp.int32).astype(jnp.float32)
+                    term = hat(place_z - offset) * plane_sum
                     total = term if total is None else total + term
                 pulled[plane, pl.ds(start, rows), pl.ds(half * lanes, lanes)] = total
             return carry
 
         lax.fori_loop(0, blocks, transport, 0)
+
+    def smooth_and_send(plane):
         for part in range(components):
             mixed = moments[part, plane].astype(jnp.float32) + pulled[plane] * grads[
                 part, plane
@@ -239,7 +257,9 @@
                 mixed.astype(jnp.bfloat16), kern[...], preferred_element_type=jnp.float32
             )
             along_y = jnp.dot(
-                kern[:height, :height], along_x.astype(jnp.bfloat16), preferred_element_type=jnp.float32
+                kern[:height, :height],
+                along_x.astype(jnp.bfloat16),
+                preferred_element_type=jnp.float32,
             ).astype(jnp.bfloat16)
             for half in range(halves):
                 outgoing[plane, :, half, part] = along_y[
@@ -247,7 +267,7 @@
                 ].reshape(blocks, rows, lanes)
 
         def send(step, carry):
-            peer = slab_peer(step)
+            peer = slab_peer(count - step)
             pltpu.make_async_remote_copy(
                 src_ref=outgoing.at[plane, peer // halves, peer % halves],
                 dst_ref=incoming.at[plane, slab],
@@ -265,17 +285,63 @@
             in_recv.at[plane],
         ).start()
 
+    def hand_on(index):
+        direct[index].wait()
+        passed[index].start()
+
+    def clear(plane):
+        @pl.when((slab == 0) | (slab == count - 1))
+        def _():
+            frame[plane] = jnp.zeros((height, breadth), jnp.bfloat16)
+
+    early, late = 1 - odd, odd
+    spread(2)
+    spread(3)
+    for load in loads[1:]:
+        load.wait()
+    gather(0, (2, 3), True)
+    hand_on(0)
+    gather(1, (2, 3), True)
+    hand_on(1)
+    spread(near[0])
+    gather(early, (near[0],), False)
+    hand_on(2)
+    hand_on(3)
+    spread(near[1])
+    gather(late, (near[1],), False)
+    passed[0].wait()
+    passed[1].wait()
+    clear(far[0])
+    spread(far[0])
+    gather(early, (near[1], far[0]), False)
+    smooth_and_send(early)
+    passed[2].wait()
+    passed[3].wait()
+    clear(far[1])
+    spread(far[1])
+    gather(late, (far[0], far[1]), False)
+    smooth_and_send(late)
+
     drain(far_grads.at[mine], grad_recv)
-    swap = pltpu.make_async_remote_copy(
-        src_ref=far_grads.at[mine],
-        dst_ref=far_grads.at[mine],
-        send_sem=swap_send,
-        recv_sem=swap_recv,
-        device_id=(partner, slab),
-        device_id_type=MESH,
-    )
-    swap.start()
-    swap.wait()
+    other = lax.rem(mine + 2, subjects)
+
+    def swap(group, index, peer):
+        return pltpu.make_async_remote_copy(
+            src_ref=far_grads.at[group],
+            dst_ref=far_grads.at[group],
+            send_sem=swap_send.at[index],
+            recv_sem=swap_recv.at[index],
+            device_id=(peer, slab),
+            device_id_type=MESH,
+        )
+
+    swaps = [swap(mine, 0, across), swap(mine, 1, partner), swap(other, 2, partner)]
+    swaps[0].start()
+    swaps[1].start()
+    swaps[0].wait()
+    swaps[2].start()
+    swaps[1].wait()
+    swaps[2].wait()
     for plane in range(depth):
         drain(incoming.at[plane], in_recv.at[plane])
 
@@ -310,22 +376,24 @@
     carry = lax.fori_loop(0, edge, advance(False), (zero, zero))
     lax.fori_loop(edge, count, advance(True), carry)
 
-    def combine(index, carry):
-        for plane in range(depth):
-            velocity = (forward[index, plane] + backward[index, plane]) * (1.0 / scale)
-            slope = far_grads[plane, index].astype(jnp.float32)
-            products[index, plane] = jnp.sum(slope * velocity, axis=0).astype(jnp.bfloat16)
+    def combine(turn, carry):
+        for group in range(subjects):
+            index = turn * subjects + group
+            for plane in range(depth):
+                velocity = (forward[index, plane] + backward[index, plane]) * (1.0 / scale)
+                slope = far_grads[group, turn, :, plane].astype(jnp.float32)
+                products[index, plane] = jnp.sum(slope * velocity, axis=0).astype(jnp.bfloat16)
         return carry
 
-    lax.fori_loop(0, count, combine, 0)
+    lax.fori_loop(0, group_size, combine, 0)
 
     def send_back(step, carry):
-        peer = slab_peer(step)
+        peer = slab_peer(count - step)
         pltpu.make_async_remote_copy(
             src_ref=products.at[peer],
             dst_ref=returned.at[slab // halves, slab % halves],
             send_sem=back_send,
-            recv_sem=back_recv,
+            recv_sem=back_recv.at[slab // group_size],
             device_id=(subject, peer),
             device_id_type=MESH,
         ).start()
@@ -333,57 +401,67 @@
 
     lax.fori_loop(1, count, send_back, 0)
     pltpu.make_async_copy(
-        products.at[slab], returned.at[slab // halves, slab % halves], back_recv
+        products.at[slab],
+        returned.at[slab // halves, slab % halves],
+        back_recv.at[slab // group_size],
     ).start()
-    drain(returned, back_recv)
 
     part_rows = height // subjects
     part_blocks = blocks // subjects
-
-    def partial(owner, plane, half):
-        block = owner * part_blocks
-        values = returned[pl.ds(block, part_blocks), half, plane]
-        values = values.reshape(part_rows, lanes).astype(jnp.float32)
+    for turn in (0, 1, subjects - 1, 2):
+        owner = lax.rem(slab // group_size + turn, subjects)
+        band_blocks = pl.ds(owner * part_blocks, part_blocks)
+        drain(returned.at[band_blocks], back_recv.at[owner])
         start = pl.multiple_of(owner * part_rows, part_rows)
-        moved = pulled[plane, pl.ds(start, part_rows), pl.ds(half * lanes, lanes)]
-        return moved * (1.0 + values)
-
-    share_copies = []
-    for step in range(1, subjects):
-        owner = lax.rem(subject + step, subjects)
+        band_rows = pl.ds(start, part_rows)
+
+        def partial(plane, half):
+            values = returned[band_blocks, half, plane].reshape(part_rows, lanes)
+            moved = pulled[plane, band_rows, pl.ds(half * lanes, lanes)]
+            return moved * (1.0 + values.astype(jnp.float32))
+
+        @pl.when(owner != subject)
+        def _():
+            slot = lax.rem(owner - subject + subjects, subjects) - 1
+            for plane in range(depth):
+                for half in range(halves):
+                    shares[slot, plane, :, pl.ds(half * lanes, lanes)] = partial(
+                        plane, half
+                    ).astype(jnp.bfloat16)
+            pltpu.make_async_remote_copy(
+                src_ref=shares.at[slot],
+                dst_ref=others.at[slot],
+                send_sem=share_send.at[slot],
+                recv_sem=share_recv.at[slot],
+                device_id=(owner, slab),
+                device_id_type=MESH,
+            ).start()
+
+        @pl.when(owner == subject)
+        def _():
+            for plane in range(depth):
+                for half in range(halves):
+                    update[plane, :, pl.ds(half * lanes, lanes)] = partial(plane, half)
+
         for plane in range(depth):
             for half in range(halves):
-                shares[step - 1, plane, :, pl.ds(half * lanes, lanes)] = partial(
-                    owner, plane, half
-                ).astype(jnp.bfloat16)
-        copy = pltpu.make_async_remote_copy(
-            src_ref=shares.at[step - 1],
-            dst_ref=others.at[step - 1],
-            send_sem=share_send.at[step - 1],
-            recv_sem=share_recv.at[step - 1],
-            device_id=(owner, slab),
-            device_id_type=MESH,
-        )
-        copy.start()
-        share_copies.append(copy)
-    for plane in range(depth):
-        for half in range(halves):
-            alignment[0, plane, :, pl.ds(half * lanes, lanes)] = returned[:, half, plane].reshape(
-                height, lanes
-            )
-    for copy in share_copies:
-        copy.wait()
-    for plane in range(depth):
-        for half in range(halves):
-            total = partial(subject, plane, half)
-            for step in range(1, subjects):
-                total = total + others[
-                    step - 1, plane, :, pl.ds(half * lanes, lanes)
-                ].astype(jnp.float32)
-            update[plane, :, pl.ds(half * lanes, lanes)] = total
+                alignment[0, plane, band_rows, pl.ds(half * lanes, lanes)] = returned[
+                    band_blocks, half, plane
+                ].reshape(part_rows, lanes)
+    for slot in range(subjects - 1):
+        drain(others.at[slot], share_recv.at[slot])
+        drain(shares.at[slot], share_send.at[slot])
+    update[...] = update[...] + sum(
+        others[slot].astype(jnp.float32) for slot in range(subjects - 1)
+    )
 
     sent = pl.ds(0, count - 1)
-    drain(far_grads.at[0, sent], grad_send)
+    drain(far_grads.at[0, pl.ds(0, group_size - 1)], grad_send)
+
+    @pl.when(jnp.logical_not(own_area))
+    def _():
+        drain(far_grads.at[0, 0], grad_send)
+
     for plane in range(depth):
         drain(incoming.at[0, sent], out_send.at[plane])
     drain(products.at[sent], back_send)
@@ -422,7 +500,7 @@
                 vmem((breadth, breadth), half),
                 vmem((depth, blocks, halves, components, rows, lanes), half),
                 vmem((depth, count, components, rows, lanes), half),
-                vmem((2, count, components, rows, lanes), half),
+                vmem((subjects, count // subjects, components, depth, rows, lanes), half),
                 vmem((count, depth, components, rows, lanes), full),
                 vmem((count, depth, components, rows, lanes), full),
                 vmem((count, depth, rows, lanes), half),
@@ -430,16 +508,16 @@
                 vmem((subjects - 1, depth, part, breadth), half),
                 vmem((subjects - 1, depth, part, breadth), half),
                 dma((4,)),
+                dma((8,)),
+                dma((8,)),
+                dma,
+                dma,
+                dma((3,)),
+                dma((3,)),
                 dma((2,)),
                 dma((2,)),
                 dma,
-                dma,
-                dma,
-                dma,
-                dma((2,)),
-                dma((2,)),
-                dma,
-                dma,
+                dma((subjects,)),
                 dma((subjects - 1,)),
                 dma((subjects - 1,)),
             ],

time: 77.7 us -> 64.8 us (0.83)
  Pallas kernels: 74.6 us -> 61.7 us
    pallas_call x1, Pallas kernels: 74.6 us -> 61.7 us  [per_device(): pl.pallas_call(body, out_shape=(jax.ShapeDtypeStruct((1, depth, height, b...]
where the time goes in v3:
time: 64.8 us; the launch traced here: 64.7 us
  Pallas kernels  61.7 us (95%)
  local copies, waits for them, and re-layouts  2.36 us (4%)
  between operations  0.65 us (1%)
    pallas_call x1, Pallas kernels, per_device(): pl.pallas_call(body, out_shape=(jax.ShapeDtypeStruct((1, depth, height, b...  61.7 us
    unnamed x4, local copies, waits for them, and re-layouts  2.36 us

profile of v3, /device:TPU:1, one launch (start us, length us, event | category | flops | bytes accessed | tf_op | source)
XLA Modules:
  0.0 64.7 jit_solution(6061807272988942428)
XLA Ops:
  0.6 61.7 %step.1 = (bf16[1,2,256,256]{3,2,1,0:T(8,128)(2,1)}, f32[2,64,256]{2,1,0:T(8,128)}) custom-call(bf16[1,3,2,256,256]{4,3,2,1,0:T(8,128)(2,1)} %refs_0_.1, bf16[1,2,256,256]{3,2,1,0:T(8,128)(2,1)} %refs_1_.1, s32[1,2,256,256]{3,2,1,0:T(8,128)} %refs_2_.1, bf16[3,2,256,256]{3,2,1,0:T(8,128)(2,1)} %refs_3_.1), custom_call_target="tpu_custom_call" | custom-call | tf_op jit(solution)/shard_map/step/pallas_call | solution.py:485
  62.3 0.0 copy-start
  62.4 1.7 %copy.8 = bf16[1,2,256,256]{3,2,1,0:T(8,128)(2,1)} copy(bf16[1,2,256,256]{3,2,1,0:T(8,128)(2,1)} %get-tuple-element.4) | data formatting | bytes 524288
  64.1 0.0 copy-done
  64.1 0.7 %copy.9 = f32[2,64,256]{2,1,0:T(8,128)} copy(f32[2,64,256]{2,1,0:T(8,128)S(1)} %copy-done) | data formatting | bytes 262144
Async XLA Ops:
  62.3 1.7 %copy-start = (f32[2,64,256]{2,1,0:T(8,128)S(1)}, f32[2,64,256]{2,1,0:T(8,128)}, u32[]{:S(2)}) copy-start(f32[2,64,256]{2,1,0:T(8,128)} %get-tuple-element.5) | copy-start | bytes 393220
